TPU v7x, 256 devices: a whole 4x4x8 slice. The times are simulated.
256 devices in a mesh: rows: 32 (over y, x, core), outs: 8 (over z).
Axes of the slice: x: 4, y: 4, z: 8, core: 2. Of those that a mesh axis runs over, the one named last changes fastest.
Arguments:
- codes: int32 [49152, 256], P('rows'), may hold values from 0 to 31
- node_of_row: int32 [49152], P('rows'), may hold values from 0 to 15
- grad: bfloat16 [49152, 128], P('rows', 'outs'), may hold values from -6 to 6
- hess: bfloat16 [49152, 128], P('rows', 'outs'), may hold values from 0.099609375 to 1
- small_side: int32 [8], replicated, may hold values from 0 to 1
- evicted: int32 [8], replicated, may hold values from 0 to 1, as said below
- parent_hist: float32 [2, 8, 128, 8192], P(None, None, 'outs', 'rows'), as said below
Outputs:
- node_hist: float32 [2, 16, 128, 8192], P(None, None, 'outs', 'rows')
- split_gain: float32 [16, 8192], P(None, 'rows')
- best_gain: float32 [16], replicated
Inputs may be any that keep to these rules, and one draw needn't show every extreme that they name: `evicted`: exactly 3 of the 8 entries are 1. `parent_hist`: the hessian component is not negative.
All inputs are finite; a program needn't handle non-finite values.
Results may differ from a plain program's by a relative error of at most 0.0003.
Values may be sent and summed in bfloat16 or wider, within the bound.
A program may use at most 256 MiB of HBM per device.

v0:
```python
import jax
import jax.numpy as jnp
from jax import lax
from jax.sharding import PartitionSpec as P

BINS = 32
TARGETS = 128


def slot_values(grads, hesses, nodes, slots):
    count = grads.shape[0]
    hit = (nodes[:, None] == slots[None, :])[:, :, None]
    grad_part = jnp.where(hit, grads[:, None, :], jnp.zeros((), grads.dtype))
    hess_part = jnp.where(hit, hesses[:, None, :], jnp.zeros((), hesses.dtype))
    return jnp.concatenate([grad_part.reshape(count, -1), hess_part.reshape(count, -1)], axis=1)


def contract(block, values):
    count = block.shape[0]
    onehot = block[:, :, None] == jnp.arange(BINS, dtype=jnp.int32)[None, None, :]
    onehot = onehot.reshape(count, -1).astype(jnp.bfloat16)
    return lax.dot_general(
        onehot, values, (((0,), (0,)), ((), ())), preferred_element_type=jnp.float32
    )


def gain_terms(node_hist):
    grads = node_hist[0]
    hesses = node_hist[1]
    nodes, targets, span = grads.shape
    grads = grads.reshape(nodes, targets, span // BINS, BINS)
    hesses = hesses.reshape(nodes, targets, span // BINS, BINS)
    left_g = jnp.cumsum(grads, axis=3)
    left_h = jnp.cumsum(hesses, axis=3)
    total_g = left_g[..., -1:]
    total_h = left_h[..., -1:]

    def score(a, s):
        return a * a / (jnp.maximum(s, 0.0) + 1.0)

    gain = (
        score(left_g, left_h) + score(total_g - left_g, total_h - left_h) - score(total_g, total_h)
    )
    return jnp.sum(gain, axis=1).reshape(nodes, span)


def local(codes, node_of_row, grad, hess, small_side, evicted, parent_hist):
    pairs = small_side.shape[0]
    local_targets = grad.shape[1]
    slots = jnp.arange(2 * pairs, dtype=jnp.int32)
    slot_count = slots.shape[0]
    span = codes.shape[1] // lax.axis_size("rows") * BINS
    values = slot_values(grad, hess, node_of_row, slots)
    built = lax.psum_scatter(contract(codes, values), "rows", scatter_dimension=0, tiled=True)
    built = jnp.transpose(built.reshape(span, 2, slot_count, local_targets), (1, 2, 3, 0))
    small = (small_side == 0)[None, :, None, None]
    pair_view = built.reshape(2, pairs, 2, local_targets, span)
    child = jnp.where(small, pair_view[:, :, 0], pair_view[:, :, 1])
    rebuilt = jnp.where(small, pair_view[:, :, 1], pair_view[:, :, 0])
    gone = (evicted == 1)[None, :, None, None]
    sibling = jnp.where(gone, rebuilt, parent_hist - child)
    first = jnp.where(small, child, sibling)
    second = jnp.where(small, sibling, child)
    node_hist = jnp.stack([first, second], axis=2).reshape(2, 2 * pairs, local_targets, span)
    partial_gain = gain_terms(node_hist)
    split_gain = lax.psum(partial_gain, "outs") / TARGETS
    best_gain = lax.pmax(jnp.max(split_gain, axis=1), "rows")
    return (node_hist, split_gain, best_gain)


def solution(mesh):
    return jax.shard_map(
        local,
        mesh=mesh,
        in_specs=(
            P("rows", None),
            P("rows"),
            P("rows", "outs"),
            P("rows", "outs"),
            P(),
            P(),
            P(None, None, "outs", "rows"),
        ),
        out_specs=(P(None, None, "outs", "rows"), P(None, "rows"), P()),
        check_vma=False,
    )
```

profile of v0, /device:TPU:1, one launch (start us, length us, event | category | flops | bytes accessed | tf_op | source)
XLA Modules:
  0.0 378.4 jit_solution(12323342735052473486)
XLA Ops:
  7.2 0.0 copy-start.3
  7.2 0.0 copy-start.2
  7.2 0.0 reduce-scatter.2.cloned.1.call-start
  7.2 0.7 iota_compare_fusion
  7.9 3.0 copy.36
  11.0 0.1 eq.47
  11.1 11.0 %bitcast_compare_fusion = pred[1536,8192]{0,1:T(32,128)(4,1)S(1)} fusion(s32[8192]{0:T(1024)S(1)} %eq.47, s32[1536,256]{0,1:T(8,128)} %copy.36), kind=kLoop, calls=%fused_computation | loop fusion | flops 12582912 | bytes 14188544 | tf_op jit(solution)/shard_map/eq | solution.py:20
  22.1 0.0 copy-done.3
  22.1 0.0 copy-done.2
  22.1 1.3 broadcast_select_fusion.1
  23.4 18.1 %fusion = f32[8192,512]{1,0:T(8,128)} fusion(pred[1536,8192]{0,1:T(32,128)(4,1)S(1)} %bitcast_compare_fusion, bf16[1536,256]{0,1:T(8,128)(2,1)} %bitcast.57, bf16[1536,256]{0,1:T(8,128)(2,1)} %bitcast.56), kind=kOutput, calls=%fused_computation.1 | convolution fusion | flops 12888047616 | bytes 30932992 | tf_op jit(solution)/shard_map/dot_general | solution.py:22
  41.5 0.0 copy-start.4
  41.5 0.0 copy-start.5
  41.5 0.0 copy-start.1
  41.5 0.0 reduce-scatter.2.cloned.1.call-update
  41.5 0.6 copy-done.4
  42.1 0.0 copy-done.5
  42.2 125.0 %reduce-scatter.2.cloned.1.call-done = f32[256,512]{1,0:T(8,128)} async-done(((f32[8192,512]{1,0:T(8,128)}), f32[256,512]{1,0:T(8,128)}) %reduce-scatter.2.cloned.1.call-update) | async-done | bytes 524304 | tf_op jit(solution)/shard_map/reduce_scatter | solution.py:54
  167.1 1.2 copy.37
  168.4 0.0 copy-done.1
  168.4 0.1 select_bitcast_fusion.1
  168.5 0.0 copy-start
  168.6 0.6 copy-done
  169.3 0.3 reshape_squeeze.6
  169.5 47.2 %reduce_window_sum.17 = f32[16,16,8,32]{3,2,1,0:T(8,128)S(1)} reduce-window(f32[16,16,8,32]{3,2,1,0:T(8,128)S(1)} %reshape_squeeze.6, f32[]{:T(128)} %constant.10.clone.1), window={size=1x1x1x32 pad=0_0x0_0x0_0x31_0}, to_apply=%region_1.2 | reduce-window | flops 2031616 | bytes 524292 | tf_op jit(solution)/shard_map/jit(cumsum)/reduce_window_sum | solution.py:33
  216.7 0.3 slice.34
  217.0 1.4 copy.48
  218.5 1.6 copy.50
  220.1 0.3 reshape_squeeze.7
  220.4 47.2 %reduce_window_sum.18 = f32[16,16,8,32]{3,2,1,0:T(8,128)S(1)} reduce-window(f32[16,16,8,32]{3,2,1,0:T(8,128)S(1)} %reshape_squeeze.7, f32[]{:T(128)} %constant.10.clone.1), window={size=1x1x1x32 pad=0_0x0_0x0_0x31_0}, to_apply=%region_2.3 | reduce-window | flops 2031616 | bytes 524292 | tf_op jit(solution)/shard_map/jit(cumsum)/reduce_window_sum | solution.py:34
  267.5 0.3 slice.35
  267.9 1.4 copy.49
  269.3 2.2 copy.51
  271.5 1.0 pad_maximum_fusion
  272.5 0.9 divide_bitcast_fusion
  273.4 0.1 copy.46
  273.5 1.8 subtract_reduce_fusion
  275.3 0.1 reshape.64
  275.4 22.7 %psum.7 = f32[16,256]{1,0:T(8,128)S(1)} all-reduce(f32[16,256]{1,0:T(8,128)S(1)} %reshape.64), channel_id=1, replica_groups=mesh['rows'=32,'outs'=8] {'outs'}, use_global_device_ids=true, to_apply=%region_4.5 | all-reduce | flops 4096 | bytes 32768 | tf_op jit(solution)/shard_map/psum | solution.py:66
  298.1 0.7 fusion.8
  298.8 71.9 %pmax.7 = f32[16]{0:T(128)} all-reduce(f32[16]{0:T(128)S(1)} %get-tuple-element.3), channel_id=1, replica_groups=mesh['rows'=32,'outs'=8] {'rows'}, use_global_device_ids=true, to_apply=%region_6.7 | all-reduce | flops 16 | bytes 128 | tf_op jit(solution)/shard_map/pmax | solution.py:67
  370.7 0.8 copy.39
  (5 shorter events, 0.1 us)
Async XLA Ops:
  7.2 14.9 %copy-start.3 = (bf16[1536,16]{0,1:T(8,128)(2,1)S(1)}, bf16[1536,16]{0,1:T(8,128)(2,1)}, u32[]{:S(2)}) copy-start(bf16[1536,16]{0,1:T(8,128)(2,1)} %param.10) | copy-start | bytes 147460
  7.2 14.9 %copy-start.2 = (bf16[1536,16]{0,1:T(8,128)(2,1)S(1)}, bf16[1536,16]{0,1:T(8,128)(2,1)}, u32[]{:S(2)}) copy-start(bf16[1536,16]{0,1:T(8,128)(2,1)} %param.9) | copy-start | bytes 147460
  7.2 160.0 %reduce-scatter.2.cloned.1.call-start = ((), (), s32[]{:S(2)}) async-start(), calls=%async_computation.1 | async-start | bytes 17301504 | tf_op jit(solution)/shard_map/reduce_scatter | solution.py:54
  41.5 0.7 copy-start.4
  41.5 0.7 copy-start.5
  41.5 126.9 %copy-start.1 = (f32[2,8,16,256]{3,2,1,0:T(8,128)S(1)}, f32[2,8,16,256]{3,2,1,0:T(8,128)}, u32[]{:S(2)}) copy-start(f32[2,8,16,256]{3,2,1,0:T(8,128)} %param.13) | copy-start | bytes 786436
  168.5 0.7 copy-start
Sparse Core Ops, SparseCore 0:
  41.6 125.4 reduce-scatter.1
where the time goes:
time: 379 us; the launch traced here: 378 us
  waiting for transfers between devices  125 us (33%)
  other arithmetic  112 us (30%)
  blocking collectives  94.6 us (25%)
  matrix products  18.1 us (5%)
  local copies, waits for them, and re-layouts  14.6 us (4%)
  between operations  14.2 us (4%)
    reduce_scatter x1, waiting for transfers between devices, local(): lax.psum_scatter(contract(codes, values), 'rows', scatter_dimension=0, ti...  125 us
    pmax x1, blocking collectives, local(): best_gain = lax.pmax(jnp.max(split_gain, axis=1), 'rows')  71.9 us
    another operation x1, other arithmetic, gain_terms(): left_g = jnp.cumsum(grads, axis=3)  47.2 us
    another operation x1, other arithmetic, gain_terms(): left_h = jnp.cumsum(hesses, axis=3)  47.2 us
    psum x1, blocking collectives, local(): split_gain = lax.psum(partial_gain, 'outs') / TARGETS  22.7 us
    dot_general x1, matrix products, contract(): lax.dot_general(onehot, values, (((0,), (0,)), ((), ())), preferred_eleme...  18.1 us
    eq x1, other arithmetic, contract(): block[:, :, None] == jnp.arange(BINS, dtype=jnp.int32)[None, None, :]  11 us
  transfers between devices with their start and end apart: 1, of which 1 were waited for; matrix products, arithmetic and copies ran while one was open for 0% of the time, Pallas kernels for 0%

commit v1 on v0

--- a/solution.py
+++ b/solution.py
@@ -63,7 +63,7 @@
     second = jnp.where(small, sibling, child)
     node_hist = jnp.stack([first, second], axis=2).reshape(2, 2 * pairs, local_targets, span)
     partial_gain = gain_terms(node_hist)
-    split_gain = lax.psum(partial_gain, "outs") / TARGETS
+    split_gain = lax.all_gather(partial_gain, "outs").sum(axis=0) / TARGETS
     best_gain = lax.pmax(jnp.max(split_gain, axis=1), "rows")
     return (node_hist, split_gain, best_gain)
 

time: 379 us -> 375 us (0.989)
  blocking collectives: 94.6 us -> 90.4 us
    psum x1 -> x0, blocking collectives: 22.7 us -> none  [local(): split_gain = lax.psum(partial_gain, 'outs') / TARGETS]
    all_gather x0 -> x1, blocking collectives: none -> 19.5 us  [local(): split_gain = lax.all_gather(partial_gain, 'outs').sum(axis=0) / TARGETS]
where the time goes in v1:
time: 375 us; the launch traced here: 374 us
  waiting for transfers between devices  125 us (33%)
  other arithmetic  112 us (30%)
  blocking collectives  90.4 us (24%)
  matrix products  18.1 us (5%)
  local copies, waits for them, and re-layouts  14.6 us (4%)
  between operations  14.2 us (4%)
    reduce_scatter x1, waiting for transfers between devices, local(): lax.psum_scatter(contract(codes, values), 'rows', scatter_dimension=0, ti...  125 us
    pmax x1, blocking collectives, local(): best_gain = lax.pmax(jnp.max(split_gain, axis=1), 'rows')  70.9 us
    another operation x1, other arithmetic, gain_terms(): left_g = jnp.cumsum(grads, axis=3)  47.2 us
    another operation x1, other arithmetic, gain_terms(): left_h = jnp.cumsum(hesses, axis=3)  47.2 us
    all_gather x1, blocking collectives, local(): split_gain = lax.all_gather(partial_gain, 'outs').sum(axis=0) / TARGETS  19.5 us
    dot_general x1, matrix products, contract(): lax.dot_general(onehot, values, (((0,), (0,)), ((), ())), preferred_eleme...  18.1 us
    eq x1, other arithmetic, contract(): block[:, :, None] == jnp.arange(BINS, dtype=jnp.int32)[None, None, :]  11 us
  transfers between devices with their start and end apart: 1, of which 1 were waited for; matrix products, arithmetic and copies ran while one was open for 0% of the time, Pallas kernels for 0%

profile of v1, /device:TPU:1, one launch (start us, length us, event | category | flops | bytes accessed | tf_op | source)
XLA Modules:
  0.0 374.3 jit_solution(9012721510448988134)
XLA Ops:
  7.2 0.0 copy-start.3
  7.2 0.0 copy-start.2
  7.2 0.0 reduce-scatter.2.cloned.1.call-start
  7.2 0.7 iota_compare_fusion
  7.9 3.0 copy.48
  11.0 0.1 eq.47
  11.1 11.0 %bitcast_compare_fusion = pred[1536,8192]{0,1:T(32,128)(4,1)S(1)} fusion(s32[8192]{0:T(1024)S(1)} %eq.47, s32[1536,256]{0,1:T(8,128)} %copy.48), kind=kLoop, calls=%fused_computation | loop fusion | flops 12582912 | bytes 14188544 | tf_op jit(solution)/shard_map/eq | solution.py:20
  22.1 0.0 copy-done.3
  22.1 0.0 copy-done.2
  22.1 1.3 broadcast_select_fusion.1
  23.4 18.1 %fusion = f32[8192,512]{1,0:T(8,128)} fusion(pred[1536,8192]{0,1:T(32,128)(4,1)S(1)} %bitcast_compare_fusion, bf16[1536,256]{0,1:T(8,128)(2,1)} %bitcast.57, bf16[1536,256]{0,1:T(8,128)(2,1)} %bitcast.56), kind=kOutput, calls=%fused_computation.1 | convolution fusion | flops 12888047616 | bytes 30932992 | tf_op jit(solution)/shard_map/dot_general | solution.py:22
  41.5 0.0 copy-start.4
  41.5 0.0 copy-start.5
  41.5 0.0 copy-start.1
  41.5 0.0 reduce-scatter.2.cloned.1.call-update
  41.5 0.6 copy-done.4
  42.1 0.0 copy-done.5
  42.2 125.0 %reduce-scatter.2.cloned.1.call-done = f32[256,512]{1,0:T(8,128)} async-done(((f32[8192,512]{1,0:T(8,128)}), f32[256,512]{1,0:T(8,128)}) %reduce-scatter.2.cloned.1.call-update) | async-done | bytes 524304 | tf_op jit(solution)/shard_map/reduce_scatter | solution.py:54
  167.1 1.2 copy.49
  168.4 0.0 copy-done.1
  168.4 0.1 select_bitcast_fusion.1
  168.5 0.0 copy-start
  168.6 0.6 copy-done
  169.3 0.3 reshape_squeeze.6
  169.5 47.2 %reduce_window_sum.17 = f32[16,16,8,32]{3,2,1,0:T(8,128)S(1)} reduce-window(f32[16,16,8,32]{3,2,1,0:T(8,128)S(1)} %reshape_squeeze.6, f32[]{:T(128)} %constant.10.clone.1), window={size=1x1x1x32 pad=0_0x0_0x0_0x31_0}, to_apply=%region_1.2 | reduce-window | flops 2031616 | bytes 524292 | tf_op jit(solution)/shard_map/jit(cumsum)/reduce_window_sum | solution.py:33
  216.7 0.3 slice.34
  217.0 1.4 copy.60
  218.5 1.6 copy.62
  220.1 0.3 reshape_squeeze.7
  220.4 47.2 %reduce_window_sum.18 = f32[16,16,8,32]{3,2,1,0:T(8,128)S(1)} reduce-window(f32[16,16,8,32]{3,2,1,0:T(8,128)S(1)} %reshape_squeeze.7, f32[]{:T(128)} %constant.10.clone.1), window={size=1x1x1x32 pad=0_0x0_0x0_0x31_0}, to_apply=%region_2.3 | reduce-window | flops 2031616 | bytes 524292 | tf_op jit(solution)/shard_map/jit(cumsum)/reduce_window_sum | solution.py:34
  267.5 0.3 slice.35
  267.9 1.4 copy.61
  269.3 2.2 copy.63
  271.5 1.0 pad_maximum_fusion
  272.5 0.9 divide_bitcast_fusion
  273.4 0.1 copy.58
  273.5 1.8 subtract_reduce_fusion
  275.3 0.1 all_gather_reshape.3
  275.4 19.5 %all_gather.3 = f32[8,16,256]{2,1,0:T(8,128)S(1)} all-gather(f32[1,16,256]{2,1,0:T(8,128)S(1)} %all_gather_reshape.3), channel_id=1, replica_groups=mesh['rows'=32,'outs'=8] {'outs'}, dimensions={0}, use_global_device_ids=true | all-gather | bytes 147456 | tf_op jit(solution)/shard_map/all_gather | solution.py:66
  294.9 0.7 fusion.8
  295.6 70.9 %pmax.7 = f32[16]{0:T(128)} all-reduce(f32[16]{0:T(128)S(1)} %get-tuple-element.3), channel_id=1, replica_groups=mesh['rows'=32,'outs'=8] {'rows'}, use_global_device_ids=true, to_apply=%region_6.7 | all-reduce | flops 16 | bytes 128 | tf_op jit(solution)/shard_map/pmax | solution.py:67
  366.6 0.8 copy.51
  (6 shorter events, 0.1 us)
Async XLA Ops:
  7.2 14.9 %copy-start.3 = (bf16[1536,16]{0,1:T(8,128)(2,1)S(1)}, bf16[1536,16]{0,1:T(8,128)(2,1)}, u32[]{:S(2)}) copy-start(bf16[1536,16]{0,1:T(8,128)(2,1)} %param.10) | copy-start | bytes 147460
  7.2 14.9 %copy-start.2 = (bf16[1536,16]{0,1:T(8,128)(2,1)S(1)}, bf16[1536,16]{0,1:T(8,128)(2,1)}, u32[]{:S(2)}) copy-start(bf16[1536,16]{0,1:T(8,128)(2,1)} %param.9) | copy-start | bytes 147460
  7.2 160.0 %reduce-scatter.2.cloned.1.call-start = ((), (), s32[]{:S(2)}) async-start(), calls=%async_computation.1 | async-start | bytes 17301504 | tf_op jit(solution)/shard_map/reduce_scatter | solution.py:54
  41.5 0.7 copy-start.4
  41.5 0.7 copy-start.5
  41.5 126.9 %copy-start.1 = (f32[2,8,16,256]{3,2,1,0:T(8,128)S(1)}, f32[2,8,16,256]{3,2,1,0:T(8,128)}, u32[]{:S(2)}) copy-start(f32[2,8,16,256]{3,2,1,0:T(8,128)} %param.13) | copy-start | bytes 786436
  168.5 0.7 copy-start
Sparse Core Ops, SparseCore 0:
  41.6 125.4 reduce-scatter.1
